TPU v7x, 128 devices: a whole 4x4x4 slice. The times are simulated.
128 devices in a mesh: gx: 8 (over y, core), gy: 4 (over z), gz: 4 (over x).
Axes of the slice: x: 4, y: 4, z: 4, core: 2. Of those that a mesh axis runs over, the one named last changes fastest.
Arguments:
- right_side: float32 [128, 64, 1024], P('gx', 'gy', 'gz'), may hold values from -8 to 8
- conductance: float32 [3, 128, 64, 1024], P(None, 'gx', 'gy', 'gz'), may hold values from 0.2 to 5
- storage: float32 [128, 64, 1024], P('gx', 'gy', 'gz'), may hold values from 0.05 to 0.8
- dirichlet: int32 [128, 64, 1024], P('gx', 'gy', 'gz'), may hold values 0 or 1
- basis: float32 [16, 128, 64, 1024], P(None, 'gx', 'gy', 'gz'), may hold values from -2 to 2
- coarse_inverse: float32 [2048, 2048], P(('gx', 'gy', 'gz')), may hold values from 0 to 2, as said below
Outputs:
- solution_field: float32 [128, 64, 1024], P('gx', 'gy', 'gz')
- residual: float32 [128, 64, 1024], P('gx', 'gy', 'gz')
Inputs may be any that keep to these rules, and one draw needn't show every extreme that they name: `coarse_inverse`: symmetric positive definite.
All inputs are finite; a program needn't handle non-finite values. No bound on the sum of `dirichlet` on one device may be relied on, other than what follows from the above.
Results may differ from a plain program's by a relative error of at most 0.0003.
Values sent between devices are 32-bit elements; how exact they have to be, the bound alone decides.
A program may use at most 128 MiB of HBM per device.

v0:
```python
import jax
import jax.numpy as jnp
from jax import lax
from jax.sharding import PartitionSpec as P

SWEEPS = 4
ITERS = 2
RELAX = 2.0 / 3.0


def padded(value, sides, width):
    for axis, dim in sides:
        count, length = (lax.axis_size(axis), value.shape[dim])
        up = [(i, (i + 1) % count) for i in range(count - 1)]
        down = [(j, i) for i, j in up]
        last = lax.slice_in_dim(value, length - width, length, axis=dim)
        leading = lax.slice_in_dim(value, 0, width, axis=dim)
        before = lax.ppermute(last, axis, up)
        after = lax.ppermute(leading, axis, down)
        value = jnp.concatenate([before, value, after], axis=dim)
    return value


def pad_cond(cond):
    return jnp.pad(cond, ((0, 0), (1, 1), (1, 1), (1, 1)))


def stencil(padded_free, padded_cond, field, storage, free):
    middle = padded_free[1:-1, 1:-1, 1:-1]
    total = storage * middle
    total = (
        total
        + padded_cond[0, 1:-1, 1:-1, 1:-1] * (middle - padded_free[2:, 1:-1, 1:-1])
        + padded_cond[0, :-2, 1:-1, 1:-1] * (middle - padded_free[:-2, 1:-1, 1:-1])
    )
    total = (
        total
        + padded_cond[1, 1:-1, 1:-1, 1:-1] * (middle - padded_free[1:-1, 2:, 1:-1])
        + padded_cond[1, 1:-1, :-2, 1:-1] * (middle - padded_free[1:-1, :-2, 1:-1])
    )
    total = (
        total
        + padded_cond[2, 1:-1, 1:-1, 1:-1] * (middle - padded_free[1:-1, 1:-1, 2:])
        + padded_cond[2, 1:-1, 1:-1, :-2] * (middle - padded_free[1:-1, 1:-1, :-2])
    )
    return free * total + (1.0 - free) * field


def diagonal_of(padded_cond, storage, free):
    total = storage + padded_cond[0, 1:-1, 1:-1, 1:-1] + padded_cond[0, :-2, 1:-1, 1:-1]
    total = total + padded_cond[1, 1:-1, 1:-1, 1:-1] + padded_cond[1, 1:-1, :-2, 1:-1]
    total = total + padded_cond[2, 1:-1, 1:-1, 1:-1] + padded_cond[2, 1:-1, 1:-1, :-2]
    return free * total + (1.0 - free)


def jacobi(rhs_box, padded_cond, diagonal, storage_box, free_box):
    guess = jnp.zeros_like(rhs_box)
    for sweep in range(SWEEPS):
        image = stencil(jnp.pad(free_box * guess, 1), padded_cond, guess, storage_box, free_box)
        guess = guess + RELAX * (rhs_box - image) / diagonal
    return guess


def project(basis, field):
    return jnp.dot(
        basis.reshape(basis.shape[0], -1), field.reshape(-1), precision=lax.Precision.HIGHEST
    )


def expand(basis, weights, field):
    return jnp.dot(
        weights, basis.reshape(basis.shape[0], -1), precision=lax.Precision.HIGHEST
    ).reshape(field.shape)


def gather_coarse(values):
    return lax.all_gather(values, ("gx", "gy", "gz"), axis=0, tiled=True)


def residual_rim(field):
    return padded(field, (("gx", 0), ("gy", 1), ("gz", 2)), 2)


def norm_sum(value):
    return lax.psum(value, ("gx", "gy", "gz"))


def shards(right_side, conductance, storage, dirichlet, basis, coarse_inverse):
    free = 1.0 - dirichlet.astype(jnp.float32)
    stacked = jnp.concatenate([conductance, storage[None], free[None]], axis=0)
    wide = padded(stacked, (("gx", 1), ("gy", 2), ("gz", 3)), 3)
    cond_face = wide[:3, 2:-2, 2:-2, 2:-2]
    free_face = wide[4, 2:-2, 2:-2, 2:-2]
    cond_box = wide[:3, 1:-1, 1:-1, 1:-1]
    storage_box = wide[3, 1:-1, 1:-1, 1:-1]
    free_box = wide[4, 1:-1, 1:-1, 1:-1]
    box_cond = pad_cond(cond_box)
    box_diag = diagonal_of(box_cond, storage_box, free_box)

    def schwarz(rhs_box):
        return jacobi(rhs_box, box_cond, box_diag, storage_box, free_box)[2:-2, 2:-2, 2:-2]

    solution = jnp.zeros_like(right_side)
    residual = right_side
    rhs_box = residual_rim(residual)
    coarse_now = project(basis, residual)
    weights = jnp.dot(coarse_inverse, gather_coarse(coarse_now), precision=lax.Precision.HIGHEST)
    precond = schwarz(rhs_box) + expand(basis, weights, residual)
    norm_now = norm_sum(jnp.sum(residual * precond))
    direction = precond
    for step in range(ITERS):
        near_dir = padded(direction, (("gx", 0), ("gy", 1), ("gz", 2)), 1)
        image = stencil(free_face * near_dir, cond_face, direction, storage, free)
        local_curve = jnp.sum(direction * image)
        curvature = lax.psum(local_curve, ("gx", "gy", "gz"))
        alpha = norm_now / curvature
        solution = solution + alpha * direction
        residual = residual - alpha * image
        if step + 1 < ITERS:
            rhs_box = residual_rim(residual)
            coarse_now = project(basis, residual)
            gathered = gather_coarse(coarse_now)
            weights = jnp.dot(coarse_inverse, gathered, precision=lax.Precision.HIGHEST)
            precond = schwarz(rhs_box) + expand(basis, weights, residual)
            norm_next = norm_sum(jnp.sum(residual * precond))
            direction = precond + norm_next / norm_now * direction
            norm_now = norm_next
    return (solution, residual)


def solution(mesh):
    placed = (
        P("gx", "gy", "gz"),
        P(None, "gx", "gy", "gz"),
        P("gx", "gy", "gz"),
        P("gx", "gy", "gz"),
        P(None, "gx", "gy", "gz"),
        P(("gx", "gy", "gz"), None),
    )
    return jax.shard_map(
        shards,
        mesh=mesh,
        in_specs=placed,
        out_specs=(P("gx", "gy", "gz"), P("gx", "gy", "gz")),
        check_vma=False,
    )
```

profile of v0, /device:TPU:1, one launch (start us, length us, event | category | flops | bytes accessed | tf_op | source)
XLA Modules:
  0.0 572.3 jit_solution(1241836847515531308)
XLA Ops:
  2.9 4.6 collective-permute-start.6
  10.3 3.6 collective-permute-start
  15.8 8.8 %fusion.8 = f32[16]{0:T(128)S(1)} fusion(f32[16,16,16,256]{3,2,1,0:T(8,128)} %param.10, f32[16,16,256,1]{2,1,0,3:T(8,128)} %bitcast.289), kind=kOutput, calls=%fused_computation.14 | convolution fusion | flops 12582912 | bytes 4456512 | tf_op jit(solution)/shard_map/dot_general | solution.py:65
  24.8 66.8 %all-reduce.8 = f32[2048]{0:T(1024)S(1)} all-reduce(f32[2048]{0:T(1024)S(1)} %dynamic-update-slice), channel_id=1, replica_groups=mesh['gx'=8,'gy'=4,'gz'=4] {'gx','gy','gz'}, use_global_device_ids=true, to_apply=%add.8 | all-reduce | flops 2048 | bytes 16384
  92.0 2.4 collective-permute-start.2
  98.7 4.7 collective-permute-start.8
  105.7 5.1 fusion.2
  110.9 8.1 %copy.37 = f32[5,22,16,256]{2,1,3,0:T(8,128)} copy(f32[5,22,16,256]{3,2,1,0:T(8,128)S(1)} %pad_maximum_fusion.2) | data formatting | bytes 3604480 | tf_op jit(solution)/shard_map/concatenate | solution.py:20
  119.0 9.0 %copy.36 = f32[5,22,3,256]{2,1,3,0:T(8,128)} copy(f32[5,22,3,256]{3,1,2,0:T(8,128)} %collective-permute-done.8) | data formatting | bytes 675840 | tf_op jit(solution)/shard_map/ppermute | solution.py:18
  128.0 9.0 %copy.38 = f32[5,22,3,256]{2,1,3,0:T(8,128)} copy(f32[5,22,3,256]{3,1,2,0:T(8,128)} %collective-permute-done.9) | data formatting | bytes 675840 | tf_op jit(solution)/shard_map/ppermute | solution.py:19
  137.0 16.9 %pad_maximum_fusion = f32[5,22,22,256]{2,1,3,0:T(8,128)S(1)} fusion(f32[5,22,3,256]{2,1,3,0:T(8,128)} %copy.38, f32[5,22,16,256]{2,1,3,0:T(8,128)} %copy.37, f32[5,22,3,256]{2,1,3,0:T(8,128)} %copy.36), kind=kLoop, calls=%fused_computation | loop fusion | flops 1239040 | bytes 4956160 | tf_op jit(solution)/shard_map/concatenate | solution.py:20
  153.8 5.4 copy-done.4
  160.0 2.7 collective-permute-start.10
  164.9 4.0 collective-permute-start.4
  170.4 9.2 %copy.40 = f32[5,22,22,256]{3,2,1,0:T(8,128)S(1)} copy(f32[5,22,22,256]{2,1,3,0:T(8,128)} %copy-done.4) | data formatting | bytes 4956160 | tf_op jit(solution)/shard_map/concatenate | solution.py:20
  179.6 3.1 copy.39
  184.6 3.2 pad_maximum_fusion.1
  191.2 3.7 fusion.213
  196.9 2.7 fusion.217
  201.5 2.1 fusion.208
  203.7 4.9 collective-permute-start.12
  208.6 2.3 collective-permute-start.13
  210.9 2.7 collective-permute-done.13
  213.7 4.3 collective-permute-start.14
  219.3 3.2 collective-permute-done.15
  222.7 4.3 collective-permute-start.16
  229.4 2.7 collective-permute-done.16
  232.2 3.9 collective-permute-done.17
  236.8 2.2 multiply_reduce_fusion.2
  239.0 63.0 %all-reduce.10 = (f32[]{:T(128)}, f32[]{:T(128)}) all-reduce(f32[]{:T(128)} %get-tuple-element.5, f32[]{:T(128)} %get-tuple-element.4), channel_id=1, replica_groups=mesh['gx'=8,'gy'=4,'gz'=4] {'gx','gy','gz'}, use_global_device_ids=true, to_apply=%region_1.2 | all-reduce | flops 2 | bytes 16 | tf_op jit(solution)/shard_map/psum | solution.py:85
  304.5 3.0 collective-permute-start.18
  309.4 8.6 %fusion.11 = f32[16]{0:T(128)S(1)} fusion(f32[16,16,16,256]{3,2,1,0:T(8,128)} %param.10, f32[16,16,256,1]{2,1,0,3:T(8,128)S(1)} %bitcast.285), kind=kOutput, calls=%fused_computation.15 | convolution fusion | flops 12582912 | bytes 4456512 | tf_op jit(solution)/shard_map/dot_general | solution.py:65
  318.3 63.0 %all-reduce.9 = f32[2048]{0:T(1024)S(1)} all-reduce(f32[2048]{0:T(1024)S(1)} %dynamic-update-slice.1), channel_id=1, replica_groups=mesh['gx'=8,'gy'=4,'gz'=4] {'gx','gy','gz'}, use_global_device_ids=true, to_apply=%add.9 | all-reduce | flops 2048 | bytes 16384
  381.4 2.7 collective-permute-start.20
  385.6 3.2 collective-permute-done.21
  392.3 6.4 %fusion = f32[1,16,16,256]{3,0,2,1:T(1,128)S(1)} fusion(f32[16,1,1,1]{0,1,3,2:T(1,128)S(1)} %convolution_bitcast_fusion, f32[16,16,256,16]{2,1,0,3:T(8,128)} %bitcast.283), kind=kOutput, calls=%fused_computation.2 | convolution fusion | flops 12582912 | bytes 4456512 | tf_op jit(solution)/shard_map/dot_general | solution.py:71
  399.5 2.0 fusion.216
  405.1 2.5 multiply_reduce_fusion.1
  407.6 67.1 %psum.30 = f32[]{:T(128)} all-reduce(f32[]{:T(128)} %get-tuple-element.10), channel_id=1, replica_groups=mesh['gx'=8,'gy'=4,'gz'=4] {'gx','gy','gz'}, use_global_device_ids=true, to_apply=%region_5.6 | all-reduce | flops 1 | bytes 8 | tf_op jit(solution)/shard_map/psum | solution.py:85
  476.9 2.3 collective-permute-start.24
  479.1 2.1 collective-permute-start.25
  481.2 3.0 collective-permute-done.25
  484.2 2.3 collective-permute-start.26
  488.0 3.2 collective-permute-done.27
  494.6 3.9 collective-permute-done.28
  498.5 3.9 collective-permute-done.29
  504.2 2.4 multiply_reduce_fusion
  506.7 63.2 %psum.31 = f32[]{:T(128)} all-reduce(f32[]{:T(128)} %get-tuple-element.8), channel_id=1, replica_groups=mesh['gx'=8,'gy'=4,'gz'=4] {'gx','gy','gz'}, use_global_device_ids=true, to_apply=%region_7.8 | all-reduce | flops 1 | bytes 8 | tf_op jit(solution)/shard_map/psum | solution.py:115
  (146 shorter events, 53.1 us)
Async XLA Ops:
  0.6 91.0 %copy-start = (f32[16,2048]{1,0:T(8,128)S(1)}, f32[16,2048]{1,0:T(8,128)}, u32[]{:S(2)}) copy-start(f32[16,2048]{1,0:T(8,128)} %param.11) | copy-start | bytes 393220
  0.6 95.8 %copy-start.15 = (f32[16,16,256]{2,1,0:T(8,128)S(1)}, f32[16,16,256]{2,1,0:T(8,128)}, u32[]{:S(2)}) copy-start(f32[16,16,256]{2,1,0:T(8,128)} %param.8) | copy-start | bytes 786436
  0.7 95.8 %copy-start.7 = (f32[3,16,16,256]{3,2,1,0:T(8,128)S(1)}, f32[3,16,16,256]{3,2,1,0:T(8,128)}, u32[]{:S(2)}) copy-start(f32[3,16,16,256]{3,2,1,0:T(8,128)} %param.7) | copy-start | bytes 2359300
  0.7 91.3 %copy-start.16 = (f32[16,16,256]{2,1,0:T(8,128)S(1)}, f32[16,16,256]{2,1,0:T(8,128)}, u32[]{:S(2)}) copy-start(f32[16,16,256]{2,1,0:T(8,128)} %param.6) | copy-start | bytes 786436
  1.8 95.9 %copy-start.18 = (f32[1,16,16,256]{3,2,1,0:T(8,128)}, f32[1,16,16,256]{3,2,1,0:T(8,128)S(1)}, u32[]{:S(2)}) copy-start(f32[1,16,16,256]{3,2,1,0:T(8,128)S(1)} %fusion.212) | copy-start | bytes 786436
  2.9 92.8 %collective-permute-start.6 = (f32[5,3,16,256]{3,2,1,0:T(8,128)S(1)}, f32[5,3,16,256]{3,2,1,0:T(8,128)S(1)}, u32[]{:S(2)}, u32[]{:S(2)}) collective-permute-start(f32[5,3,16,256]{3,2,1,0:T(8,128)S(1)} %get-tuple-element.36), channel_id=1, source_target_pairs={{0,16},{16,32},{32,48},{48,64},{64,80},{80,96},{96,112},{1,17},{17... | collective-permute-start | bytes 737288 | tf_op jit(solution)/shard_map/ppermute | solution.py:18
  7.6 88.9 %collective-permute-start.7 = (f32[5,3,16,256]{3,2,1,0:T(8,128)S(1)}, f32[5,3,16,256]{3,2,1,0:T(8,128)}, u32[]{:S(2)}, u32[]{:S(2)}) collective-permute-start(f32[5,3,16,256]{3,2,1,0:T(8,128)S(1)} %get-tuple-element.37), channel_id=1, source_target_pairs={{16,0},{32,16},{48,32},{64,48},{80,64},{96,80},{112,96},{17,1},{33... | collective-permute-start | bytes 737288 | tf_op jit(solution)/shard_map/ppermute | solution.py:19
  10.3 81.6 %collective-permute-start = (f32[2,16,256]{2,1,0:T(8,128)S(1)}, f32[2,16,256]{2,1,0:T(8,128)S(1)}, u32[]{:S(2)}, u32[]{:S(2)}) collective-permute-start(f32[2,16,256]{2,1,0:T(8,128)S(1)} %get-tuple-element.61), channel_id=1, source_target_pairs={{0,16},{16,32},{32,48},{48,64},{64,80},{80,96},{96,112},{1,17},{17... | collective-permute-start | bytes 98312 | tf_op jit(solution)/shard_map/ppermute | solution.py:18
  13.9 78.1 %collective-permute-start.1 = (f32[2,16,256]{2,1,0:T(8,128)S(1)}, f32[2,16,256]{2,1,0:T(8,128)S(1)}, u32[]{:S(2)}, u32[]{:S(2)}) collective-permute-start(f32[2,16,256]{2,1,0:T(8,128)S(1)} %get-tuple-element.60), channel_id=1, source_target_pairs={{16,0},{32,16},{48,32},{64,48},{80,64},{96,80},{112,96},{17,1},{33... | collective-permute-start | bytes 98312 | tf_op jit(solution)/shard_map/ppermute | solution.py:19
  92.0 18.8 %copy-start.22 = (f32[20,16,256]{2,1,0:T(8,128)}, f32[20,16,256]{2,1,0:T(8,128)S(1)}, u32[]{:S(2)}) copy-start(f32[20,16,256]{2,1,0:T(8,128)S(1)} %constant_dynamic-update-slice_fusion) | copy-start | bytes 983044
  92.0 18.7 %collective-permute-start.2 = (f32[20,2,256]{2,1,0:T(2,128)S(1)}, f32[20,2,256]{2,1,0:T(2,128)S(1)}, u32[]{:S(2)}, u32[]{:S(2)}) collective-permute-start(f32[20,2,256]{2,1,0:T(2,128)S(1)} %get-tuple-element.48), channel_id=1, source_target_pairs={{0,4},{4,8},{8,12},{1,5},{5,9},{9,13},{2,6},{6,10},{10,14},{3,7},{... | collective-permute-start | bytes 122888 | tf_op jit(solution)/shard_map/ppermute | solution.py:18
  94.5 16.3 %collective-permute-start.3 = (f32[20,2,256]{2,1,0:T(2,128)S(1)}, f32[20,2,256]{2,1,0:T(2,128)S(1)}, u32[]{:S(2)}, u32[]{:S(2)}) collective-permute-start(f32[20,2,256]{2,1,0:T(2,128)S(1)} %get-tuple-element.49), channel_id=1, source_target_pairs={{4,0},{8,4},{12,8},{5,1},{9,5},{13,9},{6,2},{10,6},{14,10},{7,3},{... | collective-permute-start | bytes 122888 | tf_op jit(solution)/shard_map/ppermute | solution.py:19
  98.7 20.3 %collective-permute-start.8 = (f32[5,22,3,256]{3,1,2,0:T(8,128)}, f32[5,22,3,256]{3,1,2,0:T(8,128)}, u32[]{:S(2)}, u32[]{:S(2)}) collective-permute-start(f32[5,22,3,256]{3,1,2,0:T(8,128)} %copy.55), channel_id=1, source_target_pairs={{0,4},{4,8},{8,12},{1,5},{5,9},{9,13},{2,6},{6,10},{10,14},{3,7},{... | collective-permute-start | bytes 1013768 | tf_op jit(solution)/shard_map/ppermute | solution.py:18
  104.3 23.8 %collective-permute-start.9 = (f32[5,22,3,256]{3,1,2,0:T(8,128)}, f32[5,22,3,256]{3,1,2,0:T(8,128)}, u32[]{:S(2)}, u32[]{:S(2)}) collective-permute-start(f32[5,22,3,256]{3,1,2,0:T(8,128)} %copy.56), channel_id=1, source_target_pairs={{4,0},{8,4},{12,8},{5,1},{9,5},{13,9},{6,2},{10,6},{14,10},{7,3},{... | collective-permute-start | bytes 1013768 | tf_op jit(solution)/shard_map/ppermute | solution.py:19
  160.0 19.6 %collective-permute-start.10 = (f32[5,22,22,3]{2,1,3,0:T(8,128)}, f32[5,22,22,3]{2,1,3,0:T(8,128)}, u32[]{:S(2)}, u32[]{:S(2)}) collective-permute-start(f32[5,22,22,3]{2,1,3,0:T(8,128)} %get-tuple-element.30), channel_id=1, source_target_pairs={{0,1},{1,2},{2,3},{4,5},{5,6},{6,7},{8,9},{9,10},{10,11},{12,13},{... | collective-permute-start | bytes 87128 | tf_op jit(solution)/shard_map/ppermute | solution.py:18
  162.7 20.0 %collective-permute-start.11 = (f32[5,22,22,3]{2,1,3,0:T(8,128)}, f32[5,22,22,3]{2,1,3,0:T(8,128)S(1)}, u32[]{:S(2)}, u32[]{:S(2)}) collective-permute-start(f32[5,22,22,3]{2,1,3,0:T(8,128)} %get-tuple-element.31), channel_id=1, source_target_pairs={{1,0},{2,1},{3,2},{5,4},{6,5},{7,6},{9,8},{10,9},{11,10},{13,12},{... | collective-permute-start | bytes 87128 | tf_op jit(solution)/shard_map/ppermute | solution.py:19
  164.9 25.7 %collective-permute-start.4 = (f32[20,20,2]{2,1,0:T(8,128)}, f32[20,20,2]{2,1,0:T(8,128)S(1)}, u32[]{:S(2)}, u32[]{:S(2)}) collective-permute-start(f32[20,20,2]{2,1,0:T(8,128)} %get-tuple-element.40), channel_id=1, source_target_pairs={{0,1},{1,2},{2,3},{4,5},{5,6},{6,7},{8,9},{9,10},{10,11},{12,13},{... | collective-permute-start | bytes 9608 | tf_op jit(solution)/shard_map/ppermute | solution.py:18
  168.9 22.4 %collective-permute-start.5 = (f32[20,20,2]{2,1,0:T(8,128)}, f32[20,20,2]{2,1,0:T(8,128)}, u32[]{:S(2)}, u32[]{:S(2)}) collective-permute-start(f32[20,20,2]{2,1,0:T(8,128)} %get-tuple-element.41), channel_id=1, source_target_pairs={{1,0},{2,1},{3,2},{5,4},{6,5},{7,6},{9,8},{10,9},{11,10},{13,12},{... | collective-permute-start | bytes 9608 | tf_op jit(solution)/shard_map/ppermute | solution.py:19
  187.8 48.3 %copy-start.1 = (f32[5,22,22,262]{3,2,1,0:T(8,128)}, f32[5,22,22,262]{3,2,1,0:T(8,128)S(1)}, u32[]{:S(2)}) copy-start(f32[5,22,22,262]{3,2,1,0:T(8,128)S(1)} %pad_maximum_fusion.1) | copy-start | bytes 7608484
  201.4 37.6 %copy-start.21 = (f32[20,20,260]{2,1,0:T(8,128)}, f32[20,20,260]{2,1,0:T(8,128)S(1)}, u32[]{:S(2)}) copy-start(f32[20,20,260]{2,1,0:T(8,128)S(1)} %get-tuple-element.32) | copy-start | bytes 1248004
  201.4 35.3 %copy-start.6 = (f32[5,22,22,256]{3,2,1,0:T(8,128)S(1)}, f32[5,22,22,256]{3,2,1,0:T(8,128)}, u32[]{:S(2)}) copy-start(f32[5,22,22,256]{3,2,1,0:T(8,128)} %copy-done.5) | copy-start | bytes 7434244
  201.4 35.3 %copy-start.8 = (f32[3,16,16,256]{3,2,1,0:T(8,128)S(1)}, f32[3,16,16,256]{3,2,1,0:T(8,128)}, u32[]{:S(2)}) copy-start(f32[3,16,16,256]{3,2,1,0:T(8,128)} %param.7) | copy-start | bytes 2359300
  201.4 35.3 %copy-start.12 = (f32[5,22,22,3]{3,2,1,0:T(8,128)S(1)}, f32[5,22,22,3]{3,2,1,0:T(8,128)}, u32[]{:S(2)}) copy-start(f32[5,22,22,3]{3,2,1,0:T(8,128)} %copy.39) | copy-start | bytes 87124
  201.5 35.3 %copy-start.17 = (f32[16,16,256]{2,1,0:T(8,128)S(1)}, f32[16,16,256]{2,1,0:T(8,128)}, u32[]{:S(2)}) copy-start(f32[16,16,256]{2,1,0:T(8,128)} %param.6) | copy-start | bytes 786436
  201.5 35.3 %copy-start.19 = (f32[1,16,16,256]{3,2,1,0:T(8,128)S(1)}, f32[1,16,16,256]{3,2,1,0:T(8,128)}, u32[]{:S(2)}) copy-start(f32[1,16,16,256]{3,2,1,0:T(8,128)} %copy-done.18) | copy-start | bytes 786436
  201.5 35.3 %copy-start.20 = (s32[16,16,256]{2,1,0:T(8,128)S(1)}, s32[16,16,256]{2,1,0:T(8,128)}, u32[]{:S(2)}) copy-start(s32[16,16,256]{2,1,0:T(8,128)} %param.9) | copy-start | bytes 786436
  201.5 35.3 %copy-start.26 = (f32[5,3,16,256]{3,2,1,0:T(8,128)S(1)}, f32[5,3,16,256]{3,2,1,0:T(8,128)}, u32[]{:S(2)}) copy-start(f32[5,3,16,256]{3,2,1,0:T(8,128)} %copy-done.25) | copy-start | bytes 737284
  203.7 35.4 %copy-start.10 = (f32[16,16,256]{2,1,0:T(8,128)}, f32[16,16,256]{2,1,0:T(8,128)S(1)}, u32[]{:S(2)}) copy-start(f32[16,16,256]{2,1,0:T(8,128)S(1)} %fusion.208) | copy-start | bytes 786436
  203.7 7.3 %collective-permute-start.12 = (f32[1,16,256]{2,1,0:T(8,128)S(1)}, f32[1,16,256]{2,1,0:T(8,128)S(1)}, u32[]{:S(2)}, u32[]{:S(2)}) collective-permute-start(f32[1,16,256]{2,1,0:T(8,128)S(1)} %get-tuple-element.58), channel_id=1, source_target_pairs={{0,16},{16,32},{32,48},{48,64},{64,80},{80,96},{96,112},{1,17},{17... | collective-permute-start | bytes 49160 | tf_op jit(solution)/shard_map/ppermute | solution.py:18
  208.6 5.1 collective-permute-start.13
  213.7 5.6 collective-permute-start.14
  218.0 4.5 collective-permute-start.15
  222.7 9.5 %collective-permute-start.16 = (f32[18,18,1]{2,1,0:T(8,128)S(1)}, f32[18,18,1]{2,1,0:T(8,128)S(1)}, u32[]{:S(2)}, u32[]{:S(2)}) collective-permute-start(f32[18,18,1]{2,1,0:T(8,128)S(1)} %get-tuple-element.44), channel_id=1, source_target_pairs={{0,1},{1,2},{2,3},{4,5},{5,6},{6,7},{8,9},{9,10},{10,11},{12,13},{... | collective-permute-start | bytes 3896 | tf_op jit(solution)/shard_map/ppermute | solution.py:18
  227.0 9.1 %collective-permute-start.17 = (f32[18,18,1]{2,1,0:T(8,128)S(1)}, f32[18,18,1]{2,1,0:T(8,128)S(1)}, u32[]{:S(2)}, u32[]{:S(2)}) collective-permute-start(f32[18,18,1]{2,1,0:T(8,128)S(1)} %get-tuple-element.45), channel_id=1, source_target_pairs={{1,0},{2,1},{3,2},{5,4},{6,5},{7,6},{9,8},{10,9},{11,10},{13,12},{... | collective-permute-start | bytes 3896 | tf_op jit(solution)/shard_map/ppermute | solution.py:19
  304.5 76.9 %collective-permute-start.18 = (f32[2,16,256]{2,1,0:T(8,128)S(1)}, f32[2,16,256]{2,1,0:T(8,128)S(1)}, u32[]{:S(2)}, u32[]{:S(2)}) collective-permute-start(f32[2,16,256]{2,1,0:T(8,128)S(1)} %get-tuple-element.56), channel_id=1, source_target_pairs={{0,16},{16,32},{32,48},{48,64},{64,80},{80,96},{96,112},{1,17},{17... | collective-permute-start | bytes 98312 | tf_op jit(solution)/shard_map/ppermute | solution.py:18
  307.5 73.8 %collective-permute-start.19 = (f32[2,16,256]{2,1,0:T(8,128)S(1)}, f32[2,16,256]{2,1,0:T(8,128)S(1)}, u32[]{:S(2)}, u32[]{:S(2)}) collective-permute-start(f32[2,16,256]{2,1,0:T(8,128)S(1)} %get-tuple-element.57), channel_id=1, source_target_pairs={{16,0},{32,16},{48,32},{64,48},{80,64},{96,80},{112,96},{17,1},{33... | collective-permute-start | bytes 98312 | tf_op jit(solution)/shard_map/ppermute | solution.py:19
  381.4 4.2 collective-permute-start.20
  384.1 4.7 collective-permute-start.21
  389.0 9.7 %collective-permute-start.22 = (f32[20,20,2]{2,1,0:T(8,128)S(1)}, f32[20,20,2]{2,1,0:T(8,128)S(1)}, u32[]{:S(2)}, u32[]{:S(2)}) collective-permute-start(f32[20,20,2]{2,1,0:T(8,128)S(1)} %get-tuple-element.38), channel_id=1, source_target_pairs={{0,1},{1,2},{2,3},{4,5},{5,6},{6,7},{8,9},{9,10},{10,11},{12,13},{... | collective-permute-start | bytes 9608 | tf_op jit(solution)/shard_map/ppermute | solution.py:18
  390.8 7.9 %collective-permute-start.23 = (f32[20,20,2]{2,1,0:T(8,128)S(1)}, f32[20,20,2]{2,1,0:T(8,128)S(1)}, u32[]{:S(2)}, u32[]{:S(2)}) collective-permute-start(f32[20,20,2]{2,1,0:T(8,128)S(1)} %get-tuple-element.39), channel_id=1, source_target_pairs={{1,0},{2,1},{3,2},{5,4},{6,5},{7,6},{9,8},{10,9},{11,10},{13,12},{... | collective-permute-start | bytes 9608 | tf_op jit(solution)/shard_map/ppermute | solution.py:19
  405.0 99.2 %copy-start.9 = (f32[3,16,16,256]{3,2,1,0:T(8,128)S(1)}, f32[3,16,16,256]{3,2,1,0:T(8,128)}, u32[]{:S(2)}) copy-start(f32[3,16,16,256]{3,2,1,0:T(8,128)} %param.7) | copy-start | bytes 2359300
  476.9 4.3 collective-permute-start.24
  479.1 5.1 collective-permute-start.25
  484.2 3.8 collective-permute-start.26
  486.6 84.6 %copy-start.11 = (f32[16,16,256]{2,1,0:T(8,128)S(1)}, f32[16,16,256]{2,1,0:T(8,128)}, u32[]{:S(2)}) copy-start(f32[16,16,256]{2,1,0:T(8,128)} %copy-done.10) | copy-start | bytes 786436
  486.6 4.6 collective-permute-start.27
  491.4 7.1 %collective-permute-start.28 = (f32[18,18,1]{2,1,0:T(8,128)S(1)}, f32[18,18,1]{2,1,0:T(8,128)S(1)}, u32[]{:S(2)}, u32[]{:S(2)}) collective-permute-start(f32[18,18,1]{2,1,0:T(8,128)S(1)} %get-tuple-element.42), channel_id=1, source_target_pairs={{0,1},{1,2},{2,3},{4,5},{5,6},{6,7},{8,9},{9,10},{10,11},{12,13},{... | collective-permute-start | bytes 3896 | tf_op jit(solution)/shard_map/ppermute | solution.py:18
  493.3 9.1 %collective-permute-start.29 = (f32[18,18,1]{2,1,0:T(8,128)S(1)}, f32[18,18,1]{2,1,0:T(8,128)S(1)}, u32[]{:S(2)}, u32[]{:S(2)}) collective-permute-start(f32[18,18,1]{2,1,0:T(8,128)S(1)} %get-tuple-element.43), channel_id=1, source_target_pairs={{1,0},{2,1},{3,2},{5,4},{6,5},{7,6},{9,8},{10,9},{11,10},{13,12},{... | collective-permute-start | bytes 3896 | tf_op jit(solution)/shard_map/ppermute | solution.py:19
  (14 other events, 94.5 us)
where the time goes:
time: 581 us; the launch traced here: 572 us
  blocking collectives  323 us (56%)
  starting transfers between devices  73.3 us (13%)
  local copies, waits for them, and re-layouts  55.9 us (10%)
  other arithmetic  55.2 us (10%)
  waiting for transfers between devices  29.9 us (5%)
  matrix products  29.2 us (5%)
    psum x2, blocking collectives, norm_sum(): return lax.psum(value, ('gx', 'gy', 'gz'))  130 us
    unnamed x2, blocking collectives  130 us
    psum x1, blocking collectives, shards(): curvature = lax.psum(local_curve, ('gx', 'gy', 'gz'))  63.2 us
    ppermute x15, starting transfers between devices, padded(): before = lax.ppermute(last, axis, up)  49.5 us
    ppermute x15, starting transfers between devices, padded(): after = lax.ppermute(leading, axis, down)  23.7 us
    ppermute x15, waiting for transfers between devices, padded(): after = lax.ppermute(leading, axis, down)  23.2 us
    concatenate x7, other arithmetic, padded(): value = jnp.concatenate([before, value, after], axis=dim)  21.5 us
    dot_general x2, matrix products, project(): jnp.dot(basis.reshape(basis.shape[0], -1), field.reshape(-1), precision=l...  17.4 us
  transfers between devices with their start and end apart: 30, of which 9 were waited for; matrix products, arithmetic and copies ran while one was open for 13% of the time, Pallas kernels for 0%

commit v1 on v0

--- a/solution.py
+++ b/solution.py
@@ -82,7 +82,7 @@
 
 
 def norm_sum(value):
-    return lax.psum(value, ("gx", "gy", "gz"))
+    return lax.psum(lax.psum(value, "gx"), ("gy", "gz"))
 
 
 def shards(right_side, conductance, storage, dirichlet, basis, coarse_inverse):

time: 581 us -> 614 us (1.057)
  blocking collectives: 323 us -> 353 us
    psum x1 -> x2, blocking collectives: 63.2 us -> 132 us  [shards(): curvature = lax.psum(local_curve, ('gx', 'gy', 'gz'))]
    psum x2 -> x4, blocking collectives: 130 us -> 90.6 us  [norm_sum(): return lax.psum(lax.psum(value, 'gx'), ('gy', 'gz'))]
  transfers between devices with their start and end apart: 30 -> 30, of which waited for: 9 -> 9; matrix products, arithmetic and copies ran while one was open for 13% -> 12% of each run, Pallas kernels for 0% -> 0%
where the time goes in v1:
time: 614 us; the launch traced here: 605 us
  blocking collectives  353 us (57%)
  starting transfers between devices  77.7 us (13%)
  local copies, waits for them, and re-layouts  56.2 us (9%)
  other arithmetic  55.1 us (9%)
  matrix products  29.2 us (5%)
  waiting for transfers between devices  28 us (5%)
    psum x2, blocking collectives, shards(): curvature = lax.psum(local_curve, ('gx', 'gy', 'gz'))  132 us
    unnamed x2, blocking collectives  131 us
    psum x4, blocking collectives, norm_sum(): return lax.psum(lax.psum(value, 'gx'), ('gy', 'gz'))  90.6 us
    ppermute x15, starting transfers between devices, padded(): before = lax.ppermute(last, axis, up)  52.3 us
    ppermute x15, starting transfers between devices, padded(): after = lax.ppermute(leading, axis, down)  25.3 us
    ppermute x15, waiting for transfers between devices, padded(): after = lax.ppermute(leading, axis, down)  22 us
    concatenate x7, other arithmetic, padded(): value = jnp.concatenate([before, value, after], axis=dim)  21.5 us
    dot_general x2, matrix products, project(): jnp.dot(basis.reshape(basis.shape[0], -1), field.reshape(-1), precision=l...  17.4 us
  transfers between devices with their start and end apart: 30, of which 9 were waited for; matrix products, arithmetic and copies ran while one was open for 12% of the time, Pallas kernels for 0%

profile of v1, /device:TPU:1, one launch (start us, length us, event | category | flops | bytes accessed | tf_op | source)
XLA Modules:
  0.0 605.5 jit_solution(10298334458007961743)
XLA Ops:
  2.9 4.6 collective-permute-start.6
  10.3 3.6 collective-permute-start
  15.8 8.8 %fusion.8 = f32[16]{0:T(128)S(1)} fusion(f32[16,16,16,256]{3,2,1,0:T(8,128)} %param.10, f32[16,16,256,1]{2,1,0,3:T(8,128)} %bitcast.289), kind=kOutput, calls=%fused_computation.14 | convolution fusion | flops 12582912 | bytes 4456512 | tf_op jit(solution)/shard_map/dot_general | solution.py:65
  24.8 66.8 %all-reduce.8 = f32[2048]{0:T(1024)S(1)} all-reduce(f32[2048]{0:T(1024)S(1)} %dynamic-update-slice), channel_id=1, replica_groups=mesh['gx'=8,'gy'=4,'gz'=4] {'gx','gy','gz'}, use_global_device_ids=true, to_apply=%add.8 | all-reduce | flops 2048 | bytes 16384
  92.0 2.4 collective-permute-start.2
  98.7 4.7 collective-permute-start.8
  105.7 5.1 fusion.2
  110.9 8.1 %copy.37 = f32[5,22,16,256]{2,1,3,0:T(8,128)} copy(f32[5,22,16,256]{3,2,1,0:T(8,128)S(1)} %pad_maximum_fusion.2) | data formatting | bytes 3604480 | tf_op jit(solution)/shard_map/concatenate | solution.py:20
  119.0 9.1 %copy.36 = f32[5,22,3,256]{2,1,3,0:T(8,128)} copy(f32[5,22,3,256]{3,1,2,0:T(8,128)} %collective-permute-done.8) | data formatting | bytes 675840 | tf_op jit(solution)/shard_map/ppermute | solution.py:18
  128.2 9.0 %copy.38 = f32[5,22,3,256]{2,1,3,0:T(8,128)} copy(f32[5,22,3,256]{3,1,2,0:T(8,128)} %collective-permute-done.9) | data formatting | bytes 675840 | tf_op jit(solution)/shard_map/ppermute | solution.py:19
  137.2 16.9 %pad_maximum_fusion = f32[5,22,22,256]{2,1,3,0:T(8,128)S(1)} fusion(f32[5,22,3,256]{2,1,3,0:T(8,128)} %copy.38, f32[5,22,16,256]{2,1,3,0:T(8,128)} %copy.37, f32[5,22,3,256]{2,1,3,0:T(8,128)} %copy.36), kind=kLoop, calls=%fused_computation | loop fusion | flops 1239040 | bytes 4956160 | tf_op jit(solution)/shard_map/concatenate | solution.py:20
  154.0 5.4 copy-done.4
  160.2 2.7 collective-permute-start.10
  165.1 4.0 collective-permute-start.4
  170.6 9.2 %copy.40 = f32[5,22,22,256]{3,2,1,0:T(8,128)S(1)} copy(f32[5,22,22,256]{2,1,3,0:T(8,128)} %copy-done.4) | data formatting | bytes 4956160 | tf_op jit(solution)/shard_map/concatenate | solution.py:20
  179.9 3.1 copy.39
  184.9 3.2 pad_maximum_fusion.1
  191.5 3.7 fusion.213
  197.2 2.7 fusion.217
  201.8 2.1 fusion.208
  204.0 4.9 collective-permute-start.12
  208.9 2.3 collective-permute-start.13
  211.2 2.7 collective-permute-done.13
  214.0 4.3 collective-permute-start.14
  219.6 3.2 collective-permute-done.15
  223.0 4.3 collective-permute-start.16
  229.7 2.7 collective-permute-done.16
  232.5 3.9 collective-permute-done.17
  237.1 2.1 multiply_reduce_fusion.2
  239.3 13.0 %psum.42 = f32[]{:T(128)} all-reduce(f32[]{:T(128)} %get-tuple-element.5), channel_id=1, replica_groups=mesh['gx'=8,'gy'=4,'gz'=4] {'gx'}, use_global_device_ids=true, to_apply=%region_1.2 | all-reduce | flops 1 | bytes 8 | tf_op jit(solution)/shard_map/psum | solution.py:85
  252.3 29.7 %psum.43 = f32[]{:T(128)} all-reduce(f32[]{:T(128)} %psum.42), channel_id=1, replica_groups=mesh['gx'=8,'gy'=4,'gz'=4] {'gy','gz'}, use_global_device_ids=true, to_apply=%region_2.3 | all-reduce | flops 1 | bytes 8 | tf_op jit(solution)/shard_map/psum | solution.py:85
  282.0 69.6 %psum.44 = f32[]{:T(128)} all-reduce(f32[]{:T(128)} %get-tuple-element.4), channel_id=1, replica_groups=mesh['gx'=8,'gy'=4,'gz'=4] {'gx','gy','gz'}, use_global_device_ids=true, to_apply=%region_4.5 | all-reduce | flops 1 | bytes 8 | tf_op jit(solution)/shard_map/psum | solution.py:115
  356.2 2.2 collective-permute-start.19
  358.4 8.6 %fusion.11 = f32[16]{0:T(128)S(1)} fusion(f32[16,16,16,256]{3,2,1,0:T(8,128)} %param.10, f32[16,16,256,1]{2,1,0,3:T(8,128)S(1)} %bitcast.285), kind=kOutput, calls=%fused_computation.15 | convolution fusion | flops 12582912 | bytes 4456512 | tf_op jit(solution)/shard_map/dot_general | solution.py:65
  367.3 63.8 %all-reduce.9 = f32[2048]{0:T(1024)S(1)} all-reduce(f32[2048]{0:T(1024)S(1)} %dynamic-update-slice.1), channel_id=1, replica_groups=mesh['gx'=8,'gy'=4,'gz'=4] {'gx','gy','gz'}, use_global_device_ids=true, to_apply=%add.9 | all-reduce | flops 2048 | bytes 16384
  434.6 3.2 collective-permute-done.21
  438.1 2.5 collective-permute-start.22
  442.0 6.4 %fusion = f32[1,16,16,256]{3,0,2,1:T(1,128)S(1)} fusion(f32[16,1,1,1]{0,1,3,2:T(1,128)S(1)} %convolution_bitcast_fusion, f32[16,16,256,16]{2,1,0,3:T(8,128)} %bitcast.283), kind=kOutput, calls=%fused_computation.2 | convolution fusion | flops 12582912 | bytes 4456512 | tf_op jit(solution)/shard_map/dot_general | solution.py:71
  454.8 2.5 multiply_reduce_fusion.1
  457.3 14.9 %psum.45 = f32[]{:T(128)} all-reduce(f32[]{:T(128)} %get-tuple-element.8), channel_id=1, replica_groups=mesh['gx'=8,'gy'=4,'gz'=4] {'gx'}, use_global_device_ids=true, to_apply=%region_6.7 | all-reduce | flops 1 | bytes 8 | tf_op jit(solution)/shard_map/psum | solution.py:85
  472.2 33.0 %psum.46 = f32[]{:T(128)} all-reduce(f32[]{:T(128)} %psum.45), channel_id=1, replica_groups=mesh['gx'=8,'gy'=4,'gz'=4] {'gy','gz'}, use_global_device_ids=true, to_apply=%region_7.8 | all-reduce | flops 1 | bytes 8 | tf_op jit(solution)/shard_map/psum | solution.py:85
  507.5 7.7 %collective-permute-start.24 = (f32[1,16,256]{2,1,0:T(8,128)S(1)}, f32[1,16,256]{2,1,0:T(8,128)S(1)}, u32[]{:S(2)}, u32[]{:S(2)}) collective-permute-start(f32[1,16,256]{2,1,0:T(8,128)S(1)} %get-tuple-element.52), channel_id=1, source_target_pairs={{0,16},{16,32},{32,48},{48,64},{64,80},{80,96},{96,112},{1,17},{17... | collective-permute-start | bytes 49160 | tf_op jit(solution)/shard_map/ppermute | solution.py:18
  515.2 3.1 collective-permute-start.25
  523.0 3.2 collective-permute-done.27
  529.2 3.2 collective-permute-done.28
  532.4 3.8 collective-permute-done.29
  538.0 2.4 multiply_reduce_fusion
  540.4 62.6 %psum.47 = f32[]{:T(128)} all-reduce(f32[]{:T(128)} %get-tuple-element.6), channel_id=1, replica_groups=mesh['gx'=8,'gy'=4,'gz'=4] {'gx','gy','gz'}, use_global_device_ids=true, to_apply=%region_9.10 | all-reduce | flops 1 | bytes 8 | tf_op jit(solution)/shard_map/psum | solution.py:115
  (149 shorter events, 58.3 us)
Async XLA Ops:
  0.6 91.0 %copy-start = (f32[16,2048]{1,0:T(8,128)S(1)}, f32[16,2048]{1,0:T(8,128)}, u32[]{:S(2)}) copy-start(f32[16,2048]{1,0:T(8,128)} %param.11) | copy-start | bytes 393220
  0.6 95.9 %copy-start.15 = (f32[16,16,256]{2,1,0:T(8,128)S(1)}, f32[16,16,256]{2,1,0:T(8,128)}, u32[]{:S(2)}) copy-start(f32[16,16,256]{2,1,0:T(8,128)} %param.8) | copy-start | bytes 786436
  0.7 95.8 %copy-start.7 = (f32[3,16,16,256]{3,2,1,0:T(8,128)S(1)}, f32[3,16,16,256]{3,2,1,0:T(8,128)}, u32[]{:S(2)}) copy-start(f32[3,16,16,256]{3,2,1,0:T(8,128)} %param.7) | copy-start | bytes 2359300
  0.7 91.3 %copy-start.16 = (f32[16,16,256]{2,1,0:T(8,128)S(1)}, f32[16,16,256]{2,1,0:T(8,128)}, u32[]{:S(2)}) copy-start(f32[16,16,256]{2,1,0:T(8,128)} %param.6) | copy-start | bytes 786436
  1.8 96.0 %copy-start.18 = (f32[1,16,16,256]{3,2,1,0:T(8,128)}, f32[1,16,16,256]{3,2,1,0:T(8,128)S(1)}, u32[]{:S(2)}) copy-start(f32[1,16,16,256]{3,2,1,0:T(8,128)S(1)} %fusion.212) | copy-start | bytes 786436
  2.9 92.8 %collective-permute-start.6 = (f32[5,3,16,256]{3,2,1,0:T(8,128)S(1)}, f32[5,3,16,256]{3,2,1,0:T(8,128)S(1)}, u32[]{:S(2)}, u32[]{:S(2)}) collective-permute-start(f32[5,3,16,256]{3,2,1,0:T(8,128)S(1)} %get-tuple-element.34), channel_id=1, source_target_pairs={{0,16},{16,32},{32,48},{48,64},{64,80},{80,96},{96,112},{1,17},{17... | collective-permute-start | bytes 737288 | tf_op jit(solution)/shard_map/ppermute | solution.py:18
  7.6 88.9 %collective-permute-start.7 = (f32[5,3,16,256]{3,2,1,0:T(8,128)S(1)}, f32[5,3,16,256]{3,2,1,0:T(8,128)}, u32[]{:S(2)}, u32[]{:S(2)}) collective-permute-start(f32[5,3,16,256]{3,2,1,0:T(8,128)S(1)} %get-tuple-element.35), channel_id=1, source_target_pairs={{16,0},{32,16},{48,32},{64,48},{80,64},{96,80},{112,96},{17,1},{33... | collective-permute-start | bytes 737288 | tf_op jit(solution)/shard_map/ppermute | solution.py:19
  10.3 81.6 %collective-permute-start = (f32[2,16,256]{2,1,0:T(8,128)S(1)}, f32[2,16,256]{2,1,0:T(8,128)S(1)}, u32[]{:S(2)}, u32[]{:S(2)}) collective-permute-start(f32[2,16,256]{2,1,0:T(8,128)S(1)} %get-tuple-element.59), channel_id=1, source_target_pairs={{0,16},{16,32},{32,48},{48,64},{64,80},{80,96},{96,112},{1,17},{17... | collective-permute-start | bytes 98312 | tf_op jit(solution)/shard_map/ppermute | solution.py:18
  13.9 78.1 %collective-permute-start.1 = (f32[2,16,256]{2,1,0:T(8,128)S(1)}, f32[2,16,256]{2,1,0:T(8,128)S(1)}, u32[]{:S(2)}, u32[]{:S(2)}) collective-permute-start(f32[2,16,256]{2,1,0:T(8,128)S(1)} %get-tuple-element.58), channel_id=1, source_target_pairs={{16,0},{32,16},{48,32},{64,48},{80,64},{96,80},{112,96},{17,1},{33... | collective-permute-start | bytes 98312 | tf_op jit(solution)/shard_map/ppermute | solution.py:19
  92.0 18.8 %copy-start.22 = (f32[20,16,256]{2,1,0:T(8,128)}, f32[20,16,256]{2,1,0:T(8,128)S(1)}, u32[]{:S(2)}) copy-start(f32[20,16,256]{2,1,0:T(8,128)S(1)} %constant_dynamic-update-slice_fusion) | copy-start | bytes 983044
  92.0 18.7 %collective-permute-start.2 = (f32[20,2,256]{2,1,0:T(2,128)S(1)}, f32[20,2,256]{2,1,0:T(2,128)S(1)}, u32[]{:S(2)}, u32[]{:S(2)}) collective-permute-start(f32[20,2,256]{2,1,0:T(2,128)S(1)} %get-tuple-element.46), channel_id=1, source_target_pairs={{0,4},{4,8},{8,12},{1,5},{5,9},{9,13},{2,6},{6,10},{10,14},{3,7},{... | collective-permute-start | bytes 122888 | tf_op jit(solution)/shard_map/ppermute | solution.py:18
  94.5 16.3 %collective-permute-start.3 = (f32[20,2,256]{2,1,0:T(2,128)S(1)}, f32[20,2,256]{2,1,0:T(2,128)S(1)}, u32[]{:S(2)}, u32[]{:S(2)}) collective-permute-start(f32[20,2,256]{2,1,0:T(2,128)S(1)} %get-tuple-element.47), channel_id=1, source_target_pairs={{4,0},{8,4},{12,8},{5,1},{9,5},{13,9},{6,2},{10,6},{14,10},{7,3},{... | collective-permute-start | bytes 122888 | tf_op jit(solution)/shard_map/ppermute | solution.py:19
  98.7 20.3 %collective-permute-start.8 = (f32[5,22,3,256]{3,1,2,0:T(8,128)}, f32[5,22,3,256]{3,1,2,0:T(8,128)}, u32[]{:S(2)}, u32[]{:S(2)}) collective-permute-start(f32[5,22,3,256]{3,1,2,0:T(8,128)} %copy.55), channel_id=1, source_target_pairs={{0,4},{4,8},{8,12},{1,5},{5,9},{9,13},{2,6},{6,10},{10,14},{3,7},{... | collective-permute-start | bytes 1013768 | tf_op jit(solution)/shard_map/ppermute | solution.py:18
  104.2 23.9 %collective-permute-start.9 = (f32[5,22,3,256]{3,1,2,0:T(8,128)}, f32[5,22,3,256]{3,1,2,0:T(8,128)}, u32[]{:S(2)}, u32[]{:S(2)}) collective-permute-start(f32[5,22,3,256]{3,1,2,0:T(8,128)} %copy.56), channel_id=1, source_target_pairs={{4,0},{8,4},{12,8},{5,1},{9,5},{13,9},{6,2},{10,6},{14,10},{7,3},{... | collective-permute-start | bytes 1013768 | tf_op jit(solution)/shard_map/ppermute | solution.py:19
  160.2 19.6 %collective-permute-start.10 = (f32[5,22,22,3]{2,1,3,0:T(8,128)}, f32[5,22,22,3]{2,1,3,0:T(8,128)}, u32[]{:S(2)}, u32[]{:S(2)}) collective-permute-start(f32[5,22,22,3]{2,1,3,0:T(8,128)} %get-tuple-element.28), channel_id=1, source_target_pairs={{0,1},{1,2},{2,3},{4,5},{5,6},{6,7},{8,9},{9,10},{10,11},{12,13},{... | collective-permute-start | bytes 87128 | tf_op jit(solution)/shard_map/ppermute | solution.py:18
  162.9 20.0 %collective-permute-start.11 = (f32[5,22,22,3]{2,1,3,0:T(8,128)}, f32[5,22,22,3]{2,1,3,0:T(8,128)S(1)}, u32[]{:S(2)}, u32[]{:S(2)}) collective-permute-start(f32[5,22,22,3]{2,1,3,0:T(8,128)} %get-tuple-element.29), channel_id=1, source_target_pairs={{1,0},{2,1},{3,2},{5,4},{6,5},{7,6},{9,8},{10,9},{11,10},{13,12},{... | collective-permute-start | bytes 87128 | tf_op jit(solution)/shard_map/ppermute | solution.py:19
  165.1 25.7 %collective-permute-start.4 = (f32[20,20,2]{2,1,0:T(8,128)}, f32[20,20,2]{2,1,0:T(8,128)S(1)}, u32[]{:S(2)}, u32[]{:S(2)}) collective-permute-start(f32[20,20,2]{2,1,0:T(8,128)} %get-tuple-element.38), channel_id=1, source_target_pairs={{0,1},{1,2},{2,3},{4,5},{5,6},{6,7},{8,9},{9,10},{10,11},{12,13},{... | collective-permute-start | bytes 9608 | tf_op jit(solution)/shard_map/ppermute | solution.py:18
  169.1 22.4 %collective-permute-start.5 = (f32[20,20,2]{2,1,0:T(8,128)}, f32[20,20,2]{2,1,0:T(8,128)}, u32[]{:S(2)}, u32[]{:S(2)}) collective-permute-start(f32[20,20,2]{2,1,0:T(8,128)} %get-tuple-element.39), channel_id=1, source_target_pairs={{1,0},{2,1},{3,2},{5,4},{6,5},{7,6},{9,8},{10,9},{11,10},{13,12},{... | collective-permute-start | bytes 9608 | tf_op jit(solution)/shard_map/ppermute | solution.py:19
  188.1 48.3 %copy-start.1 = (f32[5,22,22,262]{3,2,1,0:T(8,128)}, f32[5,22,22,262]{3,2,1,0:T(8,128)S(1)}, u32[]{:S(2)}) copy-start(f32[5,22,22,262]{3,2,1,0:T(8,128)S(1)} %pad_maximum_fusion.1) | copy-start | bytes 7608484
  201.7 37.6 %copy-start.21 = (f32[20,20,260]{2,1,0:T(8,128)}, f32[20,20,260]{2,1,0:T(8,128)S(1)}, u32[]{:S(2)}) copy-start(f32[20,20,260]{2,1,0:T(8,128)S(1)} %get-tuple-element.30) | copy-start | bytes 1248004
  201.7 35.3 %copy-start.6 = (f32[5,22,22,256]{3,2,1,0:T(8,128)S(1)}, f32[5,22,22,256]{3,2,1,0:T(8,128)}, u32[]{:S(2)}) copy-start(f32[5,22,22,256]{3,2,1,0:T(8,128)} %copy-done.5) | copy-start | bytes 7434244
  201.7 35.3 %copy-start.8 = (f32[3,16,16,256]{3,2,1,0:T(8,128)S(1)}, f32[3,16,16,256]{3,2,1,0:T(8,128)}, u32[]{:S(2)}) copy-start(f32[3,16,16,256]{3,2,1,0:T(8,128)} %param.7) | copy-start | bytes 2359300
  201.7 35.3 %copy-start.12 = (f32[5,22,22,3]{3,2,1,0:T(8,128)S(1)}, f32[5,22,22,3]{3,2,1,0:T(8,128)}, u32[]{:S(2)}) copy-start(f32[5,22,22,3]{3,2,1,0:T(8,128)} %copy.39) | copy-start | bytes 87124
  201.7 35.3 %copy-start.17 = (f32[16,16,256]{2,1,0:T(8,128)S(1)}, f32[16,16,256]{2,1,0:T(8,128)}, u32[]{:S(2)}) copy-start(f32[16,16,256]{2,1,0:T(8,128)} %param.6) | copy-start | bytes 786436
  201.8 35.3 %copy-start.19 = (f32[1,16,16,256]{3,2,1,0:T(8,128)S(1)}, f32[1,16,16,256]{3,2,1,0:T(8,128)}, u32[]{:S(2)}) copy-start(f32[1,16,16,256]{3,2,1,0:T(8,128)} %copy-done.18) | copy-start | bytes 786436
  201.8 35.3 %copy-start.20 = (s32[16,16,256]{2,1,0:T(8,128)S(1)}, s32[16,16,256]{2,1,0:T(8,128)}, u32[]{:S(2)}) copy-start(s32[16,16,256]{2,1,0:T(8,128)} %param.9) | copy-start | bytes 786436
  201.8 35.3 %copy-start.26 = (f32[5,3,16,256]{3,2,1,0:T(8,128)S(1)}, f32[5,3,16,256]{3,2,1,0:T(8,128)}, u32[]{:S(2)}) copy-start(f32[5,3,16,256]{3,2,1,0:T(8,128)} %copy-done.25) | copy-start | bytes 737284
  203.9 35.3 %copy-start.10 = (f32[16,16,256]{2,1,0:T(8,128)}, f32[16,16,256]{2,1,0:T(8,128)S(1)}, u32[]{:S(2)}) copy-start(f32[16,16,256]{2,1,0:T(8,128)S(1)} %fusion.208) | copy-start | bytes 786436
  204.0 7.3 %collective-permute-start.12 = (f32[1,16,256]{2,1,0:T(8,128)S(1)}, f32[1,16,256]{2,1,0:T(8,128)S(1)}, u32[]{:S(2)}, u32[]{:S(2)}) collective-permute-start(f32[1,16,256]{2,1,0:T(8,128)S(1)} %get-tuple-element.56), channel_id=1, source_target_pairs={{0,16},{16,32},{32,48},{48,64},{64,80},{80,96},{96,112},{1,17},{17... | collective-permute-start | bytes 49160 | tf_op jit(solution)/shard_map/ppermute | solution.py:18
  208.9 5.1 collective-permute-start.13
  214.0 5.6 collective-permute-start.14
  218.3 4.5 collective-permute-start.15
  223.0 9.5 %collective-permute-start.16 = (f32[18,18,1]{2,1,0:T(8,128)S(1)}, f32[18,18,1]{2,1,0:T(8,128)S(1)}, u32[]{:S(2)}, u32[]{:S(2)}) collective-permute-start(f32[18,18,1]{2,1,0:T(8,128)S(1)} %get-tuple-element.42), channel_id=1, source_target_pairs={{0,1},{1,2},{2,3},{4,5},{5,6},{6,7},{8,9},{9,10},{10,11},{12,13},{... | collective-permute-start | bytes 3896 | tf_op jit(solution)/shard_map/ppermute | solution.py:18
  227.2 9.1 %collective-permute-start.17 = (f32[18,18,1]{2,1,0:T(8,128)S(1)}, f32[18,18,1]{2,1,0:T(8,128)S(1)}, u32[]{:S(2)}, u32[]{:S(2)}) collective-permute-start(f32[18,18,1]{2,1,0:T(8,128)S(1)} %get-tuple-element.43), channel_id=1, source_target_pairs={{1,0},{2,1},{3,2},{5,4},{6,5},{7,6},{9,8},{10,9},{11,10},{13,12},{... | collective-permute-start | bytes 3896 | tf_op jit(solution)/shard_map/ppermute | solution.py:19
  354.1 77.0 %collective-permute-start.18 = (f32[2,16,256]{2,1,0:T(8,128)S(1)}, f32[2,16,256]{2,1,0:T(8,128)S(1)}, u32[]{:S(2)}, u32[]{:S(2)}) collective-permute-start(f32[2,16,256]{2,1,0:T(8,128)S(1)} %get-tuple-element.54), channel_id=1, source_target_pairs={{0,16},{16,32},{32,48},{48,64},{64,80},{80,96},{96,112},{1,17},{17... | collective-permute-start | bytes 98312 | tf_op jit(solution)/shard_map/ppermute | solution.py:18
  356.2 74.9 %collective-permute-start.19 = (f32[2,16,256]{2,1,0:T(8,128)S(1)}, f32[2,16,256]{2,1,0:T(8,128)S(1)}, u32[]{:S(2)}, u32[]{:S(2)}) collective-permute-start(f32[2,16,256]{2,1,0:T(8,128)S(1)} %get-tuple-element.55), channel_id=1, source_target_pairs={{16,0},{32,16},{48,32},{64,48},{80,64},{96,80},{112,96},{17,1},{33... | collective-permute-start | bytes 98312 | tf_op jit(solution)/shard_map/ppermute | solution.py:19
  431.1 3.5 collective-permute-start.20
  433.1 4.7 collective-permute-start.21
  438.1 10.4 %collective-permute-start.22 = (f32[20,20,2]{2,1,0:T(8,128)S(1)}, f32[20,20,2]{2,1,0:T(8,128)S(1)}, u32[]{:S(2)}, u32[]{:S(2)}) collective-permute-start(f32[20,20,2]{2,1,0:T(8,128)S(1)} %get-tuple-element.36), channel_id=1, source_target_pairs={{0,1},{1,2},{2,3},{4,5},{5,6},{6,7},{8,9},{9,10},{10,11},{12,13},{... | collective-permute-start | bytes 9608 | tf_op jit(solution)/shard_map/ppermute | solution.py:18
  440.5 7.9 %collective-permute-start.23 = (f32[20,20,2]{2,1,0:T(8,128)S(1)}, f32[20,20,2]{2,1,0:T(8,128)S(1)}, u32[]{:S(2)}, u32[]{:S(2)}) collective-permute-start(f32[20,20,2]{2,1,0:T(8,128)S(1)} %get-tuple-element.37), channel_id=1, source_target_pairs={{1,0},{2,1},{3,2},{5,4},{6,5},{7,6},{9,8},{10,9},{11,10},{13,12},{... | collective-permute-start | bytes 9608 | tf_op jit(solution)/shard_map/ppermute | solution.py:19
  454.8 83.2 %copy-start.9 = (f32[3,16,16,256]{3,2,1,0:T(8,128)S(1)}, f32[3,16,16,256]{3,2,1,0:T(8,128)}, u32[]{:S(2)}) copy-start(f32[3,16,16,256]{3,2,1,0:T(8,128)} %param.7) | copy-start | bytes 2359300
  507.5 10.8 %collective-permute-start.24 = (f32[1,16,256]{2,1,0:T(8,128)S(1)}, f32[1,16,256]{2,1,0:T(8,128)S(1)}, u32[]{:S(2)}, u32[]{:S(2)}) collective-permute-start(f32[1,16,256]{2,1,0:T(8,128)S(1)} %get-tuple-element.52), channel_id=1, source_target_pairs={{0,16},{16,32},{32,48},{48,64},{64,80},{80,96},{96,112},{1,17},{17... | collective-permute-start | bytes 49160 | tf_op jit(solution)/shard_map/ppermute | solution.py:18
  515.2 5.1 collective-permute-start.25
  520.3 2.7 collective-permute-start.26
  521.6 82.8 %copy-start.11 = (f32[16,16,256]{2,1,0:T(8,128)S(1)}, f32[16,16,256]{2,1,0:T(8,128)}, u32[]{:S(2)}) copy-start(f32[16,16,256]{2,1,0:T(8,128)} %copy-done.10) | copy-start | bytes 786436
  521.6 4.6 collective-permute-start.27
  526.4 6.0 collective-permute-start.28
  527.7 8.5 %collective-permute-start.29 = (f32[18,18,1]{2,1,0:T(8,128)S(1)}, f32[18,18,1]{2,1,0:T(8,128)S(1)}, u32[]{:S(2)}, u32[]{:S(2)}) collective-permute-start(f32[18,18,1]{2,1,0:T(8,128)S(1)} %get-tuple-element.41), channel_id=1, source_target_pairs={{1,0},{2,1},{3,2},{5,4},{6,5},{7,6},{9,8},{10,9},{11,10},{13,12},{... | collective-permute-start | bytes 3896 | tf_op jit(solution)/shard_map/ppermute | solution.py:19
  (14 other events, 94.6 us)
